TPU v7x, 32 devices: a whole 2x2x4 slice. The times are simulated.
32 devices in a mesh: lat: 8 (over y, x, core), chan: 4 (over z).
Axes of the slice: x: 2, y: 2, z: 4, core: 2. Of those that a mesh axis runs over, the one named last changes fastest.
Arguments:
- signal: bfloat16 [384, 384, 1440], P('lat', 'chan'), may hold values from -6 to 6
- spectral_filter: float32 [384, 2, 384], replicated, may hold values from -4 to 4
- channel_mix: bfloat16 [2, 384, 384], replicated, may hold values from -0.21875 to 0.21875
Outputs:
- output: bfloat16 [384, 384, 1440], P('lat', 'chan')
All inputs are finite; a program needn't handle non-finite values.
Results may differ from a plain program's by a relative error of at most 0.01.
Values may be sent and summed in bfloat16 or wider, within the bound.
No kernel may reach another device: no remote copies, remote signals or barrier semaphores. Data moves between devices by JAX's collectives and lax.ppermute only.
A program may use at most 192 MiB of HBM per device.

v0:
```python
import math
import jax
import jax.numpy as jnp
from jax import lax
from jax.sharding import PartitionSpec as P

LB = 128


def fourier_tables(orders, lon_count):
    cells = jnp.arange(lon_count, dtype=jnp.int32)
    phase = orders[:, None] * cells[None, :] % lon_count
    angle = phase.astype(jnp.float32) * (2.0 * math.pi / lon_count)
    forward = jnp.stack([jnp.cos(angle), -jnp.sin(angle)], 0)
    factor = jnp.where(orders == 0, 1.0, 2.0).astype(jnp.float32)[None, :, None]
    return (forward.astype(jnp.bfloat16), (forward * factor).astype(jnp.bfloat16))


def latitude_terms(lat_index, lat_total, lon_count):
    theta = (lat_index.astype(jnp.float32) + 0.5) * (math.pi / lat_total)
    weight = jnp.sin(theta) * (2.0 * math.pi * math.pi / (lat_total * lon_count))
    return (jnp.cos(theta), jnp.log(jnp.sin(theta)), weight)


def seed_logs(orders, log_sine):
    order_f = orders.astype(jnp.float32)[:, None]
    base_term = 0.5 * jnp.log((2.0 * order_f + 1.0) / (4.0 * math.pi))
    ratio_term = 0.5 * (
        jax.scipy.special.gammaln(order_f + 0.5)
        - jax.scipy.special.gammaln(order_f + 1.0)
        - 0.5 * math.log(math.pi)
    )
    return base_term + ratio_term + order_f * log_sine[None, :]


def legendre_rows(recursion, orders, log_seeds, first_degree, row_count, cosine):
    order_f = orders.astype(jnp.float32)[:, None]

    def advance(carried, degree):
        previous, earlier, log_scale = carried
        degree_f = degree.astype(jnp.float32)
        degree_gap = degree_f * degree_f - order_f * order_f
        coeff_a = jnp.sqrt((4.0 * degree_f * degree_f - 1.0) / jnp.maximum(degree_gap, 1.0))
        below_sq = (degree_f - 1.0) * (degree_f - 1.0)
        coeff_b = jnp.sqrt(jnp.maximum(below_sq - order_f * order_f, 0.0) / (4.0 * below_sq - 1.0))
        grown = coeff_a * (cosine[None, :] * previous - coeff_b * earlier)
        at_start = degree_f == order_f
        is_above = degree_f > order_f
        fresh_value = jnp.where(at_start, 1.0, jnp.where(is_above, grown, 0.0))
        log_scale = jnp.where(at_start, log_seeds, log_scale)
        scaled_value = fresh_value * jnp.exp(log_scale)
        rescale = jnp.where(degree_f >= order_f, jnp.abs(fresh_value) + jnp.abs(previous), 1.0)
        return (
            (fresh_value / rescale, previous / rescale, log_scale + jnp.log(rescale)),
            scaled_value,
        )

    degrees_here = first_degree + jnp.arange(row_count, dtype=jnp.int32)
    carried, values = lax.scan(advance, recursion, degrees_here, unroll=8)
    return (carried, jnp.moveaxis(values, 0, 1))


def apply_filter(coefficients, gains):
    real_part = coefficients[..., 0, :] * gains[:, 0, :] - coefficients[..., 1, :] * gains[:, 1, :]
    imag_part = coefficients[..., 0, :] * gains[:, 1, :] + coefficients[..., 1, :] * gains[:, 0, :]
    return jnp.stack([real_part, imag_part], -2)


def mix_table(channel_mix):
    real_w = channel_mix[0]
    imag_w = channel_mix[1]
    return jnp.stack([jnp.stack([real_w, imag_w], 1), jnp.stack([-imag_w, real_w], 1)], 0)


def build_legendre(orders, log_sine, cosine, first_block, degrees, lat_total):
    slot_count = orders.shape[0]
    log_seeds = seed_logs(orders, log_sine)
    zero_state = jnp.zeros((slot_count, lat_total), jnp.float32)
    empty_table = jnp.zeros((slot_count, degrees, lat_total), jnp.bfloat16)

    def build_advance_block(block_index, carried):
        recursion, legendre = carried
        recursion, block_rows = legendre_rows(
            recursion, orders, log_seeds, block_index * LB, LB, cosine
        )
        legendre = lax.dynamic_update_slice_in_dim(
            legendre, block_rows.astype(jnp.bfloat16), block_index * LB, 1
        )
        return (recursion, legendre)

    start_carry = ((zero_state, zero_state, zero_state), empty_table)
    return lax.fori_loop(first_block, degrees // LB, build_advance_block, start_carry)[1]


def analyse_rows(legendre, fourier_part, first_block, degrees):
    slot_count = legendre.shape[0]
    channel_count = fourier_part.shape[3]
    empty_sum = jnp.zeros((slot_count, degrees, 2, channel_count), jnp.float32)

    def analyse_advance_block(block_index, summed):
        block_rows = lax.dynamic_slice_in_dim(legendre, block_index * LB, LB, 1)
        partial_sum = jnp.einsum(
            "glj,gjtc->gltc", block_rows, fourier_part, preferred_element_type=jnp.float32
        )
        return lax.dynamic_update_slice_in_dim(summed, partial_sum, block_index * LB, 1)

    return lax.fori_loop(first_block, degrees // LB, analyse_advance_block, empty_sum)


def synthesise_rows(legendre, mixed_part, first_block, degrees):
    slot_count, _, lat_total = legendre.shape
    channel_count = mixed_part.shape[3]
    empty_sum = jnp.zeros((slot_count, lat_total, 2, channel_count), jnp.float32)

    def synthesise_advance_block(block_index, summed):
        block_rows = lax.dynamic_slice_in_dim(legendre, block_index * LB, LB, 1)
        block_values = lax.dynamic_slice_in_dim(mixed_part, block_index * LB, LB, 1)
        return summed + jnp.einsum(
            "glj,gltc->gjtc", block_rows, block_values, preferred_element_type=jnp.float32
        )

    return lax.fori_loop(first_block, degrees // LB, synthesise_advance_block, empty_sum)


def on_device(signal, spectral_filter, channel_mix):
    lat_count = lax.axis_size("lat")
    chan_count = lax.axis_size("chan")
    lat_rows, quarter, lon_count = signal.shape
    lat_total = lat_rows * lat_count
    degrees = spectral_filter.shape[0]
    full_channels = channel_mix.shape[1]
    per_dev = degrees // lat_count
    sub_count = per_dev // chan_count
    lat_index = lax.axis_index("lat")
    chan_index = lax.axis_index("chan")
    every_slot = jnp.arange(degrees, dtype=jnp.int32)
    dest_dev = every_slot // per_dev
    slot_index = every_slot % per_dev
    own_slots = chan_index * sub_count + jnp.arange(sub_count, dtype=jnp.int32)
    orders_all = dest_dev * per_dev + slot_index
    orders_own = lat_index * per_dev + own_slots
    trig, synth = fourier_tables(orders_all, lon_count)
    own_rows = lat_index * lat_rows + jnp.arange(lat_rows, dtype=jnp.int32)
    _, _, own_weight = latitude_terms(own_rows, lat_total, lon_count)
    spectrum = jnp.einsum("acn,tkn->katc", signal, trig, preferred_element_type=jnp.float32)
    spectrum = (spectrum * own_weight[None, :, None, None]).astype(jnp.bfloat16)
    fourier = lax.all_to_all(
        lax.all_to_all(spectrum, "lat", split_axis=0, concat_axis=1, tiled=True),
        "chan",
        split_axis=0,
        concat_axis=3,
        tiled=True,
    )
    cosine, log_sine, _ = latitude_terms(
        jnp.arange(lat_total, dtype=jnp.int32), lat_total, lon_count
    )
    slot_total = orders_own.shape[0]
    first_end = slot_total // 2
    bounds = [(0, first_end), (first_end, slot_total)]
    tables = []
    first_blocks = []
    filtered_parts = []
    for start_slot, end_slot in bounds:
        group_orders = orders_own[start_slot:end_slot]
        first_block = jnp.min(group_orders) // LB
        legendre = build_legendre(group_orders, log_sine, cosine, first_block, degrees, lat_total)
        fourier_part = fourier[start_slot:end_slot]
        coefficients = analyse_rows(legendre, fourier_part, first_block, degrees)
        filtered_parts.append(apply_filter(coefficients, spectral_filter).astype(jnp.bfloat16))
        tables.append(legendre)
        first_blocks.append(first_block)
    filtered = jnp.concatenate(filtered_parts, 0)
    kernel = mix_table(channel_mix)
    flat_kernel = kernel.reshape(2 * full_channels, 2 * full_channels)
    mixed = jnp.dot(
        filtered.reshape(slot_total * degrees, 2 * full_channels),
        flat_kernel,
        preferred_element_type=jnp.float32,
    )
    mixed = mixed.astype(jnp.bfloat16).reshape(slot_total, degrees, 2, full_channels)
    back_parts = []
    for group_index in range(len(bounds)):
        start_slot, end_slot = bounds[group_index]
        mixed_part = mixed[start_slot:end_slot]
        back_parts.append(
            synthesise_rows(tables[group_index], mixed_part, first_blocks[group_index], degrees)
        )
    back = jnp.concatenate(back_parts, 0).astype(jnp.bfloat16)
    back = lax.all_to_all(back, "chan", split_axis=3, concat_axis=0, tiled=True)
    returned = lax.all_to_all(back, "lat", split_axis=1, concat_axis=0, tiled=True)
    output = jnp.einsum("katc,tkn->acn", returned, synth, preferred_element_type=jnp.float32)
    return output.astype(jnp.bfloat16)


def solution(mesh):
    return jax.shard_map(
        on_device,
        mesh=mesh,
        in_specs=(P("lat", "chan", None), P(), P()),
        out_specs=P("lat", "chan", None),
        check_vma=False,
    )
```

profile of v0, /device:TPU:0, one launch (start us, length us, event | category | flops | bytes accessed | tf_op | source)
XLA Modules:
  0.0 1342.0 jit_solution(16196962002320569169)
XLA Ops:
  0.0 10.2 fusion.40
  10.3 17.6 %fusion.27 = bf16[384,48,2,96]{0,3,1,2:T(8,128)(2,1)} fusion(f32[48]{0:T(128)S(1)} %sine_multiply_fusion, bf16[48,96,1440]{2,1,0:T(8,128)(2,1)} %param.19, f32[1,384,1440]{1,2,0:T(8,128)} %get-tuple-element.1470, f32[1,384,1440]{1,2,0:T(8,128)S(1)} %get-tuple-element.1469), kind=kOutput, calls=%fused_computation.192 | convolution fusion | flops 10203660288 | bytes 24772800 | tf_op jit(solution)/shard_map/acn,tkn->katc/dot_general | solution.py:145
  27.9 11.8 copy.33
  39.7 5.2 all-to-all-start
  48.7 331.1 %while.159 = (s32[]{:T(128)}, f32[6,384]{1,0:T(8,128)S(1)}, f32[6,384]{1,0:T(8,128)S(1)}, f32[6,384]{1,0:T(8,128)S(1)}, bf16[6,384,384]{2,0,1:T(8,128)(2,1)S(1)}...) while((s32[]{:T(128)}, f32[6,384]{1,0:T(8,128)S(1)}, ...), condition=%wide.region_4.5_spmd.clone.clone, body=%wide.region_1.4_spmd.clone.clone.sunk | while | flops 430591 | bytes 2527546 | solution.py:92
  48.9 110.0 %while.162 = (s32[]{:T(128)}, f32[6,384]{1,0:T(8,128)S(1)}, f32[6,384]{1,0:T(8,128)S(1)}, f32[6,384]{1,0:T(8,128)S(1)}, bf16[16,8,6,384]{3,2,1,0:T(8,128)(2,1)S(...) while((s32[]{:T(128)}, f32[6,384]{1,0:T(8,128)S(1)}, ...), condition=%wide.region_3.3_spmd.clone, body=%wide.region_2.2_spmd.clone.sunk | while | flops 424441 | bytes 941511 | solution.py:59
  159.2 110.0 %while.162 = (s32[]{:T(128)}, f32[6,384]{1,0:T(8,128)S(1)}, f32[6,384]{1,0:T(8,128)S(1)}, f32[6,384]{1,0:T(8,128)S(1)}, bf16[16,8,6,384]{3,2,1,0:T(8,128)(2,1)S(...) while((s32[]{:T(128)}, f32[6,384]{1,0:T(8,128)S(1)}, ...), condition=%wide.region_3.3_spmd.clone, body=%wide.region_2.2_spmd.clone.sunk | while | flops 424441 | bytes 941511 | solution.py:59
  269.6 110.0 %while.162 = (s32[]{:T(128)}, f32[6,384]{1,0:T(8,128)S(1)}, f32[6,384]{1,0:T(8,128)S(1)}, f32[6,384]{1,0:T(8,128)S(1)}, bf16[16,8,6,384]{3,2,1,0:T(8,128)(2,1)S(...) while((s32[]{:T(128)}, f32[6,384]{1,0:T(8,128)S(1)}, ...), condition=%wide.region_3.3_spmd.clone, body=%wide.region_2.2_spmd.clone.sunk | while | flops 424441 | bytes 941511 | solution.py:59
  382.6 10.2 copy.34
  392.8 11.4 copy.35
  404.2 6.2 all-to-all-start.1
  410.7 320.8 %while.161 = (s32[]{:T(128)}, f32[6,384]{1,0:T(8,128)S(1)}, f32[6,384]{1,0:T(8,128)S(1)}, f32[6,384]{1,0:T(8,128)S(1)}, bf16[6,384,384]{2,0,1:T(8,128)(2,1)S(1)}...) while((s32[]{:T(128)}, f32[6,384]{1,0:T(8,128)S(1)}, ...), condition=%wide.region_11.12_spmd.clone.clone, body=%wide.region_8.11_spmd.clone.clone.sunk | while | flops 430591 | bytes 2527546 | solution.py:92
  411.0 106.5 %while.163 = (s32[]{:T(128)}, f32[6,384]{1,0:T(8,128)S(1)}, f32[6,384]{1,0:T(8,128)S(1)}, f32[6,384]{1,0:T(8,128)S(1)}, bf16[16,8,6,384]{3,2,1,0:T(8,128)(2,1)S(...) while((s32[]{:T(128)}, f32[6,384]{1,0:T(8,128)S(1)}, ...), condition=%wide.region_10.10_spmd.clone, body=%wide.region_9.9_spmd.clone.sunk | while | flops 424441 | bytes 941511 | solution.py:59
  517.9 106.5 %while.163 = (s32[]{:T(128)}, f32[6,384]{1,0:T(8,128)S(1)}, f32[6,384]{1,0:T(8,128)S(1)}, f32[6,384]{1,0:T(8,128)S(1)}, bf16[16,8,6,384]{3,2,1,0:T(8,128)(2,1)S(...) while((s32[]{:T(128)}, f32[6,384]{1,0:T(8,128)S(1)}, ...), condition=%wide.region_10.10_spmd.clone, body=%wide.region_9.9_spmd.clone.sunk | while | flops 424441 | bytes 941511 | solution.py:59
  624.8 106.5 %while.163 = (s32[]{:T(128)}, f32[6,384]{1,0:T(8,128)S(1)}, f32[6,384]{1,0:T(8,128)S(1)}, f32[6,384]{1,0:T(8,128)S(1)}, bf16[16,8,6,384]{3,2,1,0:T(8,128)(2,1)S(...) while((s32[]{:T(128)}, f32[6,384]{1,0:T(8,128)S(1)}, ...), condition=%wide.region_10.10_spmd.clone, body=%wide.region_9.9_spmd.clone.sunk | while | flops 424441 | bytes 941511 | solution.py:59
  731.5 3.2 copy.37
  734.7 4.2 copy.46
  738.9 1.4 copy.42
  740.3 2.6 copy.49
  744.6 1.2 copy.69
  747.9 5.9 fusion.71
  753.8 2.3 copy.36
  756.1 4.5 copy.38
  760.7 3.6 broadcast.1824.clone.1
  764.3 9.8 while.154
  764.3 3.2 convolution_dynamic-update-slice_fusion.4
  767.6 3.2 convolution_dynamic-update-slice_fusion.4
  770.8 3.2 convolution_dynamic-update-slice_fusion.4
  774.1 4.3 copy.41
  778.3 4.5 copy.43
  782.9 3.5 broadcast.1824.clone.2
  786.4 10.0 while.155
  786.4 3.2 convolution_dynamic-update-slice_fusion.5
  789.7 3.2 convolution_dynamic-update-slice_fusion.5
  792.9 3.3 convolution_dynamic-update-slice_fusion.5
  796.4 6.5 subtract_convert_fusion.1
  803.9 68.3 %copy.44 = bf16[12,384,2,384]{3,2,1,0:T(2,128)(2,1)S(1)} copy(bf16[12,384,2,384]{3,1,2,0:T(8,128)(2,1)S(1)} %maximum_maximum_fusion) | data formatting | bytes 14155776 | tf_op jit(solution)/shard_map/concatenate | solution.py:172
  872.2 1.2 copy.68
  873.4 7.2 convolution_convert_fusion
  880.6 3.4 fusion.70
  884.0 6.6 slice.191
  890.6 3.6 broadcast.1824.clone.3
  894.3 24.2 %while.156 = (s32[]{:T(128)}, f32[6,384,2,384]{3,1,2,0:T(8,128)}, bf16[6,384,384]{1,2,0:T(8,128)(2,1)}, bf16[6,384,2,384]{3,2,1,0:T(2,128)(2,1)S(1)}, s32[]{:T(128)}, /*index=5*/s32[]{:T(128)}, s32[]{:T(128)}, s32[]{:T(128)}) while((s32[]{:T(128)}, f32[6,384,2,384]{3,1,2,0:T(8,128)}, bf16[6,384,384]{1,2,0:T(8,128)(2,1)}, ...), condition=%wide.region_15.16_spmd, body=%wide.region_14.15_spmd.sunk | while | flops 454754304 | bytes 18284684 | solution.py:122
  895.1 7.3 convolution_add_fusion.4
  903.2 7.3 convolution_add_fusion.4
  911.2 7.3 convolution_add_fusion.4
  918.5 12.9 copy.48
  931.4 6.6 slice.193
  938.0 3.6 broadcast.1824.clone
  941.6 24.6 %while.157 = (s32[]{:T(128)}, f32[6,384,2,384]{3,1,2,0:T(8,128)}, bf16[6,384,384]{1,2,0:T(8,128)(2,1)}, bf16[6,384,2,384]{3,2,1,0:T(2,128)(2,1)S(1)}, s32[]{:T(128)}, /*index=5*/s32[]{:T(128)}, s32[]{:T(128)}, s32[]{:T(128)}) while((s32[]{:T(128)}, f32[6,384,2,384]{3,1,2,0:T(8,128)}, bf16[6,384,384]{1,2,0:T(8,128)(2,1)}, ...), condition=%wide.region_17.18_spmd, body=%wide.region_16.17_spmd.sunk | while | flops 454754304 | bytes 18284684 | solution.py:122
  942.9 7.3 convolution_add_fusion.5
  950.9 7.3 convolution_add_fusion.5
  959.0 7.3 convolution_add_fusion.5
  966.3 13.1 copy.51
  979.4 18.3 %pad_maximum_fusion = bf16[12,384,2,384]{1,2,0,3:T(2,128)(2,1)S(1)} fusion(bf16[6,384,2,384]{1,2,0,3:T(2,128)(2,1)} %copy.51, bf16[6,384,2,384]{1,2,0,3:T(2,128)(2,1)S(1)} %copy-done.1), kind=kLoop, calls=%fused_computation.194 | loop fusion | flops 3538944 | bytes 14155776 | tf_op jit(solution)/shard_map/concatenate | solution.py:188
  997.7 160.6 %all_to_all.69 = bf16[12,384,2,384]{1,2,0,3:T(2,128)(2,1)S(1)} all-to-all(bf16[12,384,2,384]{1,2,0,3:T(2,128)(2,1)S(1)} %pad_maximum_fusion), channel_id=1, replica_groups=mesh['lat'=8,'chan'=4] {'chan'}, dimensions={3} | all-to-all | bytes 14155776 | tf_op jit(solution)/shard_map/all_to_all | solution.py:189
  1158.3 1.3 copy.52
  1159.6 4.3 copy.53
  1163.9 20.6 %copy.54 = bf16[48,384,2,96]{3,2,0,1:T(2,128)(2,1)} copy(bf16[48,384,2,96]{1,3,2,0:T(8,128)(2,1)} %bitcast.405) | data formatting | bytes 14155776 | tf_op jit(solution)/shard_map/all_to_all | solution.py:189
  1184.5 5.1 all-to-all-start.3
  1189.5 105.3 %all-to-all-done.3 = bf16[48,384,2,96]{3,2,0,1:T(2,128)(2,1)} async-done(((bf16[48,384,2,96]{3,2,0,1:T(2,128)(2,1)}), bf16[48,384,2,96]{3,2,0,1:T(2,128)(2,1)}, u32[]{:S(2)}, u32[]{:S(2)}) %all-to-all-start.3) | async-done | bytes 7077920 | tf_op jit(solution)/shard_map/all_to_all | solution.py:190
  1294.8 11.1 copy.55
  1305.9 9.3 copy.56
  1315.2 26.6 %bitcast_convert_fusion = bf16[48,96,1440]{2,1,0:T(8,128)(2,1)} fusion(bf16[384,48,2,96]{3,1,2,0:T(8,128)(2,1)} %bitcast.410, f32[1,384,1440]{1,2,0:T(8,128)} %get-tuple-element.1470, f32[1,384,1440]{1,2,0:T(8,128)S(1)} %copy-done.3, f32[384]{0:T(512)S(1)} %compare_select_fusion.4), kind=kOutput, calls=%fused_computation.186 | convolution fusion | flops 10202112000 | bytes 24774144 | tf_op jit(solution)/shard_map/katc,tkn->acn/dot_general | solution.py:191
  (1513 shorter events, 177.2 us)
Async XLA Ops:
  10.2 17.7 %copy-start.2 = (f32[1,384,1440]{1,2,0:T(8,128)}, f32[1,384,1440]{1,2,0:T(8,128)S(1)}, u32[]{:S(2)}) copy-start(f32[1,384,1440]{1,2,0:T(8,128)S(1)} %get-tuple-element.1469) | copy-start | bytes 6635524
  39.7 342.9 %all-to-all-start = ((bf16[384,48,2,96]{3,1,2,0:T(8,128)(2,1)}), bf16[384,48,2,96]{3,1,2,0:T(8,128)(2,1)}, u32[]{:S(2)}, u32[]{:S(2)}) async-start(bf16[384,48,2,96]{3,1,2,0:T(8,128)(2,1)} %copy.33), calls=%async_computation | async-start | bytes 18874368 | tf_op jit(solution)/shard_map/all_to_all | solution.py:148
  379.8 13.1 copy-start
  404.2 343.6 %all-to-all-start.1 = ((bf16[48,384,2,96]{1,3,2,0:T(8,128)(2,1)}), bf16[48,384,2,96]{1,3,2,0:T(8,128)(2,1)}, u32[]{:S(2)}, u32[]{:S(2)}) async-start(bf16[48,384,2,96]{1,3,2,0:T(8,128)(2,1)} %copy.35), calls=%async_computation.1 | async-start | bytes 14155776 | tf_op jit(solution)/shard_map/all_to_all | solution.py:147
  738.9 4.1 copy-start.4
  743.2 2.6 copy-start.5
  966.3 13.1 copy-start.1
  1184.5 110.4 %all-to-all-start.3 = ((bf16[48,384,2,96]{3,2,0,1:T(2,128)(2,1)}), bf16[48,384,2,96]{3,2,0,1:T(2,128)(2,1)}, u32[]{:S(2)}, u32[]{:S(2)}) async-start(bf16[48,384,2,96]{3,2,0,1:T(2,128)(2,1)} %copy.54), calls=%async_computation.3 | async-start | bytes 18874368 | tf_op jit(solution)/shard_map/all_to_all | solution.py:190
  1305.9 9.3 copy-start.3
where the time goes:
time: 1360 us; the launch traced here: 1340 us
  loops' own time  486 us (36%)
  local copies, waits for them, and re-layouts  318 us (23%)
  blocking collectives  161 us (12%)
  other arithmetic  135 us (10%)
  matrix products  114 us (8%)
  waiting for transfers between devices  105 us (8%)
  starting transfers between devices  16.5 us (1%)
    another operation x6, loops' own time, legendre_rows(): carried, values = lax.scan(advance, recursion, degrees_here, unroll=8)  485 us
    all_to_all x1, blocking collectives, on_device(): back = lax.all_to_all(back, 'chan', split_axis=3, concat_axis=0, tiled=True)  161 us
    all_to_all x1, waiting for transfers between devices, on_device(): lax.all_to_all(back, 'lat', split_axis=1, concat_axis=0, tiled=True)  105 us
    while x672, other arithmetic  68.7 us
    concatenate x1, local copies, waits for them, and re-layouts, on_device(): filtered = jnp.concatenate(filtered_parts, 0)  68.3 us
    slice x96, local copies, waits for them, and re-layouts, legendre_rows(): carried, values = lax.scan(advance, recursion, degrees_here, unroll=8)  58.7 us
    dot_general x6, matrix products, synthesise_advance_block(): jnp.einsum('glj,gltc->gjtc', block_rows, block_values, preferred_element_...  43.5 us
    while x4, local copies, waits for them, and re-layouts, synthesise_rows(): lax.fori_loop(first_block, degrees // LB, synthesise_advance_block, empty...  32.8 us
  transfers between devices with their start and end apart: 3, of which 1 were waited for; matrix products, arithmetic and copies ran while one was open for 14% of the time, Pallas kernels for 0%

commit v1 on v0

--- a/solution.py
+++ b/solution.py
@@ -144,13 +144,20 @@
     _, _, own_weight = latitude_terms(own_rows, lat_total, lon_count)
     spectrum = jnp.einsum("acn,tkn->katc", signal, trig, preferred_element_type=jnp.float32)
     spectrum = (spectrum * own_weight[None, :, None, None]).astype(jnp.bfloat16)
-    fourier = lax.all_to_all(
-        lax.all_to_all(spectrum, "lat", split_axis=0, concat_axis=1, tiled=True),
-        "chan",
-        split_axis=0,
-        concat_axis=3,
-        tiled=True,
-    )
+    array = lax.all_to_all(spectrum, "lat", split_axis=0, concat_axis=1, tiled=True)
+    ways, here = (lax.axis_size("chan"), lax.axis_index("chan"))
+    width = array.shape[0] // ways
+    shape = list(array.shape)
+    shape[0] = width
+    height = shape[3]
+    shape[3] = height * ways
+    full = jnp.zeros(shape, array.dtype)
+    for mask in range(ways):
+        part = lax.dynamic_slice_in_dim(array, (here ^ mask) * width, width, axis=0)
+        if mask:
+            part = lax.ppermute(part, "chan", [(d, d ^ mask) for d in range(ways)])
+        full = lax.dynamic_update_slice_in_dim(full, part, (here ^ mask) * height, axis=3)
+    fourier = full
     cosine, log_sine, _ = latitude_terms(
         jnp.arange(lat_total, dtype=jnp.int32), lat_total, lon_count
     )

time: 1360 us -> 1450 us (1.066)
  local copies, waits for them, and re-layouts: 318 us -> 401 us
    dynamic_update_slice x0 -> x4, local copies, waits for them, and re-layouts: none -> 73.2 us  [on_device(): lax.dynamic_update_slice_in_dim(full, part, (here ^ mask) * height, axis=3)]
    dynamic_slice x0 -> x4, local copies, waits for them, and re-layouts: none -> 19.9 us  [on_device(): part = lax.dynamic_slice_in_dim(array, (here ^ mask) * width, width, axis=0)]
  transfers between devices with their start and end apart: 3 -> 5, of which waited for: 1 -> 1; matrix products, arithmetic and copies ran while one was open for 14% -> 18% of each run, Pallas kernels for 0% -> 0%
where the time goes in v1:
time: 1450 us; the launch traced here: 1430 us
  loops' own time  494 us (34%)
  local copies, waits for them, and re-layouts  401 us (28%)
  blocking collectives  159 us (11%)
  other arithmetic  135 us (9%)
  matrix products  118 us (8%)
  waiting for transfers between devices  105 us (7%)
  starting transfers between devices  15.8 us (1%)
    another operation x6, loops' own time, legendre_rows(): carried, values = lax.scan(advance, recursion, degrees_here, unroll=8)  485 us
    all_to_all x1, blocking collectives, on_device(): back = lax.all_to_all(back, 'chan', split_axis=3, concat_axis=0, tiled=True)  159 us
    all_to_all x1, waiting for transfers between devices, on_device(): lax.all_to_all(back, 'lat', split_axis=1, concat_axis=0, tiled=True)  105 us
    dynamic_update_slice x4, local copies, waits for them, and re-layouts, on_device(): lax.dynamic_update_slice_in_dim(full, part, (here ^ mask) * height, axis=3)  73.2 us
    while x672, other arithmetic  68.7 us
    concatenate x1, local copies, waits for them, and re-layouts, on_device(): filtered = jnp.concatenate(filtered_parts, 0)  68.3 us
    slice x96, local copies, waits for them, and re-layouts, legendre_rows(): carried, values = lax.scan(advance, recursion, degrees_here, unroll=8)  59.1 us
    dot_general x6, matrix products, synthesise_advance_block(): jnp.einsum('glj,gltc->gjtc', block_rows, block_values, preferred_element_...  43.5 us
  transfers between devices with their start and end apart: 5, of which 1 were waited for; matrix products, arithmetic and copies ran while one was open for 18% of the time, Pallas kernels for 0%

profile of v1, /device:TPU:0, one launch (start us, length us, event | category | flops | bytes accessed | tf_op | source)
XLA Modules:
  0.0 1434.6 jit_solution(6373741635568239589)
XLA Ops:
  0.0 10.2 fusion.40
  10.3 17.6 %fusion.27 = bf16[384,48,2,96]{0,3,1,2:T(8,128)(2,1)} fusion(f32[48]{0:T(128)S(1)} %sine_multiply_fusion, bf16[48,96,1440]{2,1,0:T(8,128)(2,1)} %param.19, f32[1,384,1440]{1,2,0:T(8,128)} %get-tuple-element.1490, f32[1,384,1440]{1,2,0:T(8,128)S(1)} %get-tuple-element.1489), kind=kOutput, calls=%fused_computation.192 | convolution fusion | flops 10203660288 | bytes 24772800 | tf_op jit(solution)/shard_map/acn,tkn->katc/dot_general | solution.py:145
  27.9 11.8 copy.46
  39.7 5.2 all-to-all-start
  48.6 329.8 %while.161 = (s32[]{:T(128)}, f32[6,384]{1,0:T(8,128)S(1)}, f32[6,384]{1,0:T(8,128)S(1)}, f32[6,384]{1,0:T(8,128)S(1)}, bf16[6,384,384]{2,0,1:T(8,128)(2,1)S(1)}...) while((s32[]{:T(128)}, f32[6,384]{1,0:T(8,128)S(1)}, ...), condition=%wide.region_11.12_spmd.clone.clone, body=%wide.region_8.11_spmd.clone.clone.sunk | while | flops 430591 | bytes 2527546 | solution.py:92
  48.8 109.5 %while.163 = (s32[]{:T(128)}, f32[6,384]{1,0:T(8,128)S(1)}, f32[6,384]{1,0:T(8,128)S(1)}, f32[6,384]{1,0:T(8,128)S(1)}, bf16[16,8,6,384]{3,2,1,0:T(8,128)(2,1)S(...) while((s32[]{:T(128)}, f32[6,384]{1,0:T(8,128)S(1)}, ...), condition=%wide.region_10.10_spmd.clone, body=%wide.region_9.9_spmd.clone.sunk | while | flops 424441 | bytes 941511 | solution.py:59
  158.6 109.5 %while.163 = (s32[]{:T(128)}, f32[6,384]{1,0:T(8,128)S(1)}, f32[6,384]{1,0:T(8,128)S(1)}, f32[6,384]{1,0:T(8,128)S(1)}, bf16[16,8,6,384]{3,2,1,0:T(8,128)(2,1)S(...) while((s32[]{:T(128)}, f32[6,384]{1,0:T(8,128)S(1)}, ...), condition=%wide.region_10.10_spmd.clone, body=%wide.region_9.9_spmd.clone.sunk | while | flops 424441 | bytes 941511 | solution.py:59
  268.5 109.5 %while.163 = (s32[]{:T(128)}, f32[6,384]{1,0:T(8,128)S(1)}, f32[6,384]{1,0:T(8,128)S(1)}, f32[6,384]{1,0:T(8,128)S(1)}, bf16[16,8,6,384]{3,2,1,0:T(8,128)(2,1)S(...) while((s32[]{:T(128)}, f32[6,384]{1,0:T(8,128)S(1)}, ...), condition=%wide.region_10.10_spmd.clone, body=%wide.region_9.9_spmd.clone.sunk | while | flops 424441 | bytes 941511 | solution.py:59
  381.0 10.2 copy.47
  391.3 7.7 constant_dynamic-slice_fusion.4
  399.0 4.1 copy.48
  403.1 3.0 collective-permute-start
  406.1 4.1 copy.50
  412.7 4.1 copy.52
  418.4 324.8 %while.159 = (s32[]{:T(128)}, f32[6,384]{1,0:T(8,128)S(1)}, f32[6,384]{1,0:T(8,128)S(1)}, f32[6,384]{1,0:T(8,128)S(1)}, bf16[6,384,384]{2,0,1:T(8,128)(2,1)}, /*...) while((s32[]{:T(128)}, f32[6,384]{1,0:T(8,128)S(1)}, ...), condition=%wide.region_4.5_spmd.clone.clone, body=%wide.region_1.4_spmd.clone.clone.sunk | while | flops 430591 | bytes 2330938 | solution.py:92
  418.6 107.1 %while.162 = (s32[]{:T(128)}, f32[6,384]{1,0:T(8,128)S(1)}, f32[6,384]{1,0:T(8,128)S(1)}, f32[6,384]{1,0:T(8,128)S(1)}, bf16[16,8,6,384]{3,2,1,0:T(8,128)(2,1)S(...) while((s32[]{:T(128)}, f32[6,384]{1,0:T(8,128)S(1)}, ...), condition=%wide.region_3.3_spmd.clone, body=%wide.region_2.2_spmd.clone.sunk | while | flops 424441 | bytes 941511 | solution.py:59
  526.8 107.1 %while.162 = (s32[]{:T(128)}, f32[6,384]{1,0:T(8,128)S(1)}, f32[6,384]{1,0:T(8,128)S(1)}, f32[6,384]{1,0:T(8,128)S(1)}, bf16[16,8,6,384]{3,2,1,0:T(8,128)(2,1)S(...) while((s32[]{:T(128)}, f32[6,384]{1,0:T(8,128)S(1)}, ...), condition=%wide.region_3.3_spmd.clone, body=%wide.region_2.2_spmd.clone.sunk | while | flops 424441 | bytes 941511 | solution.py:59
  635.1 107.1 %while.162 = (s32[]{:T(128)}, f32[6,384]{1,0:T(8,128)S(1)}, f32[6,384]{1,0:T(8,128)S(1)}, f32[6,384]{1,0:T(8,128)S(1)}, bf16[16,8,6,384]{3,2,1,0:T(8,128)(2,1)S(...) while((s32[]{:T(128)}, f32[6,384]{1,0:T(8,128)S(1)}, ...), condition=%wide.region_3.3_spmd.clone, body=%wide.region_2.2_spmd.clone.sunk | while | flops 424441 | bytes 941511 | solution.py:59
  743.2 3.1 copy.54
  746.3 4.2 copy.60
  759.7 4.0 broadcast_in_dim.705
  763.7 15.4 %dynamic_update_slice.47 = bf16[12,384,2,384]{3,1,2,0:T(8,128)(2,1)} dynamic-update-slice(bf16[12,384,2,384]{3,1,2,0:T(8,128)(2,1)} %broadcast_in_dim.705, bf16[12,384,2,96]{3,1,2,0:T(8,128)(2,1)S(1)} %copy-done.1, s32[]{:T(128)} %constant.384.clone.1, s32[]{:T(128)} %constant.384.clone.1, s32[]{:T(128)} %constant.384.clone.1, s32[]{:T(128)S(6)} %select_n.518) | dynamic-update-slice | bytes 3538948 | tf_op jit(solution)/shard_map/dynamic_update_slice | solution.py:159
  782.0 19.5 %dynamic_update_slice.48 = bf16[12,384,2,384]{3,1,2,0:T(8,128)(2,1)} dynamic-update-slice(bf16[12,384,2,384]{3,1,2,0:T(8,128)(2,1)} %dynamic_update_slice.47, bf16[12,384,2,96]{3,1,2,0:T(8,128)(2,1)S(1)} %copy.49, s32[]{:T(128)} %constant.384.clone.1, s32[]{:T(128)} %constant.384.clone.1, s32[]{:T(128)} %constant.384.clone.1, s32[]{:T(128)S(6)} %select_n.520) | dynamic-update-slice | bytes 3538948 | tf_op jit(solution)/shard_map/dynamic_update_slice | solution.py:159
  804.4 19.5 %dynamic_update_slice.49 = bf16[12,384,2,384]{3,1,2,0:T(8,128)(2,1)} dynamic-update-slice(bf16[12,384,2,384]{3,1,2,0:T(8,128)(2,1)} %dynamic_update_slice.48, bf16[12,384,2,96]{3,1,2,0:T(8,128)(2,1)S(1)} %copy.51, s32[]{:T(128)} %constant.384.clone.1, s32[]{:T(128)} %constant.384.clone.1, s32[]{:T(128)} %constant.384.clone.1, s32[]{:T(128)S(6)} %select_n.522) | dynamic-update-slice | bytes 3538948 | tf_op jit(solution)/shard_map/dynamic_update_slice | solution.py:159
  823.9 2.9 copy.53
  826.9 18.7 %dynamic_update_slice.50 = bf16[12,384,2,384]{3,1,2,0:T(8,128)(2,1)} dynamic-update-slice(bf16[12,384,2,384]{3,1,2,0:T(8,128)(2,1)} %dynamic_update_slice.49, bf16[12,384,2,96]{3,1,2,0:T(8,128)(2,1)S(1)} %copy.53, s32[]{:T(128)} %constant.384.clone.1, s32[]{:T(128)} %constant.384.clone.1, s32[]{:T(128)} %constant.384.clone.1, s32[]{:T(128)S(6)} %select_n.524) | dynamic-update-slice | bytes 3538948 | tf_op jit(solution)/shard_map/dynamic_update_slice | solution.py:159
  845.6 5.8 fusion.71
  851.4 3.6 broadcast.1826.clone.2
  854.9 13.2 while.155
  854.9 4.4 convolution_dynamic-update-slice_fusion.5
  859.3 4.4 convolution_dynamic-update-slice_fusion.5
  863.7 4.4 convolution_dynamic-update-slice_fusion.5
  868.1 3.6 broadcast.1826.clone.1
  871.8 18.1 %while.154 = (s32[]{:T(128)}, f32[6,384,2,384]{3,1,2,0:T(8,128)}, bf16[6,384,384]{2,1,0:T(8,128)(2,1)}, bf16[6,384,2,384]{3,1,2,0:T(8,128)(2,1)S(1)}, s32[]{:T(128)}, /*index=5*/s32[]{:T(128)}, s32[]{:T(128)}, s32[]{:T(128)}) while((s32[]{:T(128)}, f32[6,384,2,384]{3,1,2,0:T(8,128)}, bf16[6,384,384]{2,1,0:T(8,128)(2,1)}, ...), condition=%wide.region_6.7_spmd, body=%wide.region_5.6_spmd.sunk | while | flops 452984832 | bytes 6489219 | solution.py:107
  871.8 3.2 convolution_dynamic-update-slice_fusion.4
  875.0 3.2 convolution_dynamic-update-slice_fusion.4
  878.3 3.2 convolution_dynamic-update-slice_fusion.4
  889.9 6.5 subtract_convert_fusion.1
  897.5 68.3 %copy.58 = bf16[12,384,2,384]{3,2,1,0:T(2,128)(2,1)S(1)} copy(bf16[12,384,2,384]{3,1,2,0:T(8,128)(2,1)S(1)} %maximum_maximum_fusion) | data formatting | bytes 14155776 | tf_op jit(solution)/shard_map/concatenate | solution.py:179
  967.0 7.2 convolution_convert_fusion
  974.2 3.4 fusion.70
  977.5 6.6 slice.183
  984.1 3.6 broadcast.1826.clone.3
  987.8 24.2 %while.156 = (s32[]{:T(128)}, f32[6,384,2,384]{3,1,2,0:T(8,128)}, bf16[6,384,384]{1,2,0:T(8,128)(2,1)}, bf16[6,384,2,384]{3,2,1,0:T(2,128)(2,1)S(1)}, s32[]{:T(128)}, /*index=5*/s32[]{:T(128)}, s32[]{:T(128)}, s32[]{:T(128)}) while((s32[]{:T(128)}, f32[6,384,2,384]{3,1,2,0:T(8,128)}, bf16[6,384,384]{1,2,0:T(8,128)(2,1)}, ...), condition=%wide.region_15.16_spmd, body=%wide.region_14.15_spmd.sunk | while | flops 454754304 | bytes 18284684 | solution.py:122
  988.6 7.3 convolution_add_fusion.4
  996.7 7.3 convolution_add_fusion.4
  1004.7 7.3 convolution_add_fusion.4
  1012.0 12.9 copy.62
  1024.9 6.6 slice.185
  1031.5 3.6 broadcast.1826.clone
  1035.2 24.4 %while.157 = (s32[]{:T(128)}, f32[6,384,2,384]{3,1,2,0:T(8,128)}, bf16[6,384,384]{1,2,0:T(8,128)(2,1)}, bf16[6,384,2,384]{3,2,1,0:T(2,128)(2,1)S(1)}, s32[]{:T(128)}, /*index=5*/s32[]{:T(128)}, s32[]{:T(128)}, s32[]{:T(128)}) while((s32[]{:T(128)}, f32[6,384,2,384]{3,1,2,0:T(8,128)}, bf16[6,384,384]{1,2,0:T(8,128)(2,1)}, ...), condition=%wide.region_17.18_spmd, body=%wide.region_16.17_spmd.sunk | while | flops 454754304 | bytes 18284684 | solution.py:122
  1036.2 7.3 convolution_add_fusion.5
  1044.3 7.3 convolution_add_fusion.5
  1052.3 7.3 convolution_add_fusion.5
  1059.6 13.1 copy.65
  1072.7 18.3 %pad_maximum_fusion = bf16[12,384,2,384]{1,2,0,3:T(2,128)(2,1)S(1)} fusion(bf16[6,384,2,384]{1,2,0,3:T(2,128)(2,1)} %copy.65, bf16[6,384,2,384]{1,2,0,3:T(2,128)(2,1)S(1)} %copy-done), kind=kLoop, calls=%fused_computation.194 | loop fusion | flops 3538944 | bytes 14155776 | tf_op jit(solution)/shard_map/concatenate | solution.py:195
  1091.0 159.5 %all_to_all.54 = bf16[12,384,2,384]{1,2,0,3:T(2,128)(2,1)S(1)} all-to-all(bf16[12,384,2,384]{1,2,0,3:T(2,128)(2,1)S(1)} %pad_maximum_fusion), channel_id=1, replica_groups=mesh['lat'=8,'chan'=4] {'chan'}, dimensions={3} | all-to-all | bytes 14155776 | tf_op jit(solution)/shard_map/all_to_all | solution.py:196
  1251.8 4.3 copy.67
  1256.1 20.6 %copy.68 = bf16[48,384,2,96]{3,2,0,1:T(2,128)(2,1)} copy(bf16[48,384,2,96]{1,3,2,0:T(8,128)(2,1)} %bitcast.400) | data formatting | bytes 14155776 | tf_op jit(solution)/shard_map/all_to_all | solution.py:196
  1276.7 5.1 all-to-all-start.2
  1281.8 105.3 %all-to-all-done.2 = bf16[48,384,2,96]{3,2,0,1:T(2,128)(2,1)} async-done(((bf16[48,384,2,96]{3,2,0,1:T(2,128)(2,1)}), bf16[48,384,2,96]{3,2,0,1:T(2,128)(2,1)}, u32[]{:S(2)}, u32[]{:S(2)}) %all-to-all-start.2) | async-done | bytes 7077920 | tf_op jit(solution)/shard_map/all_to_all | solution.py:197
  1387.1 11.1 copy.69
  1398.1 9.3 copy.70
  1407.5 26.7 %bitcast_convert_fusion = bf16[48,96,1440]{2,1,0:T(8,128)(2,1)} fusion(bf16[384,48,2,96]{3,1,2,0:T(8,128)(2,1)} %bitcast.403, f32[1,384,1440]{1,2,0:T(8,128)} %get-tuple-element.1490, f32[1,384,1440]{1,2,0:T(8,128)S(1)} %copy-done.3, f32[384]{0:T(512)S(1)} %compare_select_fusion.4), kind=kOutput, calls=%fused_computation.186 | convolution fusion | flops 10202112000 | bytes 24774144 | tf_op jit(solution)/shard_map/katc,tkn->acn/dot_general | solution.py:198
  (1524 shorter events, 198.0 us)
Async XLA Ops:
  10.2 17.7 %copy-start.2 = (f32[1,384,1440]{1,2,0:T(8,128)}, f32[1,384,1440]{1,2,0:T(8,128)S(1)}, u32[]{:S(2)}) copy-start(f32[1,384,1440]{1,2,0:T(8,128)S(1)} %get-tuple-element.1489) | copy-start | bytes 6635524
  39.7 341.3 %all-to-all-start = ((bf16[384,48,2,96]{3,1,2,0:T(8,128)(2,1)}), bf16[384,48,2,96]{3,1,2,0:T(8,128)(2,1)}, u32[]{:S(2)}, u32[]{:S(2)}) async-start(bf16[384,48,2,96]{3,1,2,0:T(8,128)(2,1)} %copy.46), calls=%async_computation | async-start | bytes 18874368 | tf_op jit(solution)/shard_map/all_to_all | solution.py:147
  403.1 376.0 %collective-permute-start = (bf16[12,384,2,96]{1,3,2,0:T(8,128)(2,1)}, bf16[12,384,2,96]{1,3,2,0:T(8,128)(2,1)}, u32[]{:S(2)}, u32[]{:S(2)}) collective-permute-start(bf16[12,384,2,96]{1,3,2,0:T(8,128)(2,1)} %copy.48), channel_id=1, source_target_pairs={{0,1},{1,0},{2,3},{3,2},{4,5},{5,4},{6,7},{7,6},{8,9},{9,8},{10,11... | collective-permute-start | bytes 5308424 | tf_op jit(solution)/shard_map/ppermute | solution.py:158
  410.1 391.4 %collective-permute-start.1 = (bf16[12,384,2,96]{1,3,2,0:T(8,128)(2,1)}, bf16[12,384,2,96]{1,3,2,0:T(8,128)(2,1)}, u32[]{:S(2)}, u32[]{:S(2)}) collective-permute-start(bf16[12,384,2,96]{1,3,2,0:T(8,128)(2,1)} %copy.50), channel_id=1, source_target_pairs={{0,2},{1,3},{2,0},{3,1},{4,6},{5,7},{6,4},{7,5},{8,10},{9,11},{10,... | collective-permute-start | bytes 5308424 | tf_op jit(solution)/shard_map/ppermute | solution.py:158
  416.8 407.2 %collective-permute-start.2 = (bf16[12,384,2,96]{1,3,2,0:T(8,128)(2,1)}, bf16[12,384,2,96]{1,3,2,0:T(8,128)(2,1)}, u32[]{:S(2)}, u32[]{:S(2)}) collective-permute-start(bf16[12,384,2,96]{1,3,2,0:T(8,128)(2,1)} %copy.52), channel_id=1, source_target_pairs={{0,3},{1,2},{2,1},{3,0},{4,7},{5,6},{6,5},{7,4},{8,11},{9,10},{10,... | collective-permute-start | bytes 5308424 | tf_op jit(solution)/shard_map/ppermute | solution.py:158
  750.5 4.2 copy-start.4
  754.9 2.6 copy-start.5
  759.7 4.0 copy-start.1
  1059.6 13.1 copy-start
  1276.7 110.4 %all-to-all-start.2 = ((bf16[48,384,2,96]{3,2,0,1:T(2,128)(2,1)}), bf16[48,384,2,96]{3,2,0,1:T(2,128)(2,1)}, u32[]{:S(2)}, u32[]{:S(2)}) async-start(bf16[48,384,2,96]{3,2,0,1:T(2,128)(2,1)} %copy.68), calls=%async_computation.2 | async-start | bytes 18874368 | tf_op jit(solution)/shard_map/all_to_all | solution.py:197
  1398.1 9.3 copy-start.3
